TPU v7x, 32 devices: a whole 2x2x4 slice. The times are simulated.
32 devices in a mesh: grp: 4 (over x, core), mem: 8 (over z, y).
Axes of the slice: x: 2, y: 2, z: 4, core: 2. Of those that a mesh axis runs over, the one named last changes fastest.
Arguments:
- amplitudes: bfloat16 [384, 262144], P('mem', 'grp'), may hold values from -6 to 6
- integrals: bfloat16 [262144, 1024], P(('grp', 'mem')), may hold values from -0.0625 to 0.0625
- irrep_ef: int32 [262144], P(('grp', 'mem')), may hold values from 0 to 7
- irrep_ab: int32 [1024], replicated, may hold values from 0 to 7
Outputs:
- residual: float32 [384, 1024], P('mem', 'grp')
All inputs are finite; a program needn't handle non-finite values.
Results may differ from a plain program's by a relative error of at most 0.0003.
Values may be sent and summed in bfloat16 or wider, within the bound.
No kernel may reach another device: no remote copies, remote signals or barrier semaphores. Data moves between devices by JAX's collectives and lax.ppermute only.
A program may use at most 128 MiB of HBM per device.

v0:
```python
import jax
import jax.numpy as jnp
from jax import lax
from jax.sharding import PartitionSpec as P


def local(amplitudes, integrals, irrep_ef, irrep_ab):
    member_count = lax.axis_size("mem")
    own_rows = amplitudes.shape[0]
    pair_cols = integrals.shape[0]
    allowed = irrep_ef[:, None] == irrep_ab[None, :]
    blocked = jnp.where(allowed, integrals, jnp.zeros_like(integrals))
    shaped = amplitudes.reshape(own_rows, member_count, pair_cols)
    arrived = lax.all_to_all(shaped, "mem", split_axis=1, concat_axis=0, tiled=True)
    partial_value = jnp.dot(
        arrived.reshape(-1, pair_cols), blocked, preferred_element_type=jnp.float32
    )
    row_share = lax.psum_scatter(partial_value, "mem", scatter_dimension=0, tiled=True)
    result = lax.psum_scatter(row_share, "grp", scatter_dimension=1, tiled=True)
    return result


def solution(mesh):
    placed = (P("mem", "grp"), P(("grp", "mem"), None), P(("grp", "mem")), P())
    return jax.shard_map(
        local, mesh=mesh, in_specs=placed, out_specs=P("mem", "grp"), check_vma=False
    )
```

profile of v0, /device:TPU:0, one launch (start us, length us, event | category | flops | bytes accessed | tf_op | source)
XLA Modules:
  0.0 271.0 jit_solution(445686489094129673)
XLA Ops:
  6.5 0.0 reduce-scatter.7.cloned.1.call-start
  6.5 3.2 %copy.15 = bf16[6,8,8,8192]{3,2,0,1:T(8,128)(2,1)S(1)} copy(bf16[6,8,8,8192]{3,2,1,0:T(8,128)(2,1)} %bitcast.14) | data formatting | bytes 12582912 | tf_op jit(solution)/shard_map/reshape | solution.py:13
  9.7 0.0 copy-start
  9.7 0.0 copy-start.1
  9.8 145.3 %all_to_all.15 = bf16[48,8,8192]{2,0,1:T(8,128)(2,1)} all-to-all(bf16[48,8,8192]{2,0,1:T(8,128)(2,1)S(1)} %bitcast.13), channel_id=1, replica_groups=mesh['grp'=4,'mem'=8] {'mem'}, dimensions={1} | all-to-all | bytes 12582912 | tf_op jit(solution)/shard_map/all_to_all | solution.py:14
  155.1 0.0 copy-done
  155.1 0.0 copy-done.1
  155.1 17.7 %fusion.4 = f32[384,1024]{0,1:T(8,128)S(1)} fusion(bf16[384,8192]{1,0:T(8,128)(2,1)} %bitcast.15, bf16[8192,1024]{1,0:T(8,128)(2,1)} %param.5, s32[1024]{0:T(1024)S(1)} %copy-done.1, s32[8192]{0:T(1024)S(1)} %copy-done), kind=kOutput, calls=%fused_computation.6 | convolution fusion | flops 6459228160 | bytes 24678400 | tf_op jit(solution)/shard_map/dot_general | solution.py:15
  172.8 1.6 copy.11
  174.4 0.0 reduce-scatter.7.cloned.1.call-update
  174.5 0.0 reduce-scatter.5.cloned.1.call-start
  174.5 65.1 %reduce-scatter.7.cloned.1.call-done = f32[48,1024]{1,0:T(8,128)} async-done(((f32[384,1024]{1,0:T(8,128)}), f32[48,1024]{1,0:T(8,128)}) %reduce-scatter.7.cloned.1.call-update) | async-done | bytes 196624
  239.6 1.9 copy.12
  241.5 0.0 reduce-scatter.5.cloned.1.call-update
  241.5 21.0 %reduce-scatter.5.cloned.1.call-done = f32[48,256]{0,1:T(8,128)} async-done(((f32[48,1024]{0,1:T(8,128)}), f32[48,256]{0,1:T(8,128)}) %reduce-scatter.5.cloned.1.call-update) | async-done | bytes 49168 | tf_op jit(solution)/shard_map/reduce_scatter | solution.py:19
  262.5 1.6 copy.10
Async XLA Ops:
  6.5 233.0 %reduce-scatter.7.cloned.1.call-start = ((), (), s32[]{:S(2)}) async-start(), calls=%async_computation.4 | async-start | bytes 1769472
  9.7 145.4 %copy-start = (s32[8192]{0:T(1024)S(1)}, s32[8192]{0:T(1024)}, u32[]{:S(2)}) copy-start(s32[8192]{0:T(1024)} %param.6) | copy-start | bytes 98308
  9.7 145.3 %copy-start.1 = (s32[1024]{0:T(1024)S(1)}, s32[1024]{0:T(1024)}, u32[]{:S(2)}) copy-start(s32[1024]{0:T(1024)} %param.7) | copy-start | bytes 12292
  174.5 88.1 %reduce-scatter.5.cloned.1.call-start = ((), (), s32[]{:S(2)}) async-start(), calls=%async_computation.3 | async-start | bytes 655360 | tf_op jit(solution)/shard_map/reduce_scatter | solution.py:19
Sparse Core Ops, SparseCore 0:
  174.6 64.9 reduce-scatter.6
  242.1 20.4 reduce-scatter.4
where the time goes:
time: 271 us
  blocking collectives  145 us (54%)
  waiting for transfers between devices  86.1 us (32%)
  matrix products  17.7 us (7%)
  between operations  13.4 us (5%)
  local copies, waits for them, and re-layouts  8.38 us (3%)
    all_to_all x1, blocking collectives, local(): lax.all_to_all(shaped, 'mem', split_axis=1, concat_axis=0, tiled=True)  145 us
    unnamed x3, waiting for transfers between devices  65.1 us
    reduce_scatter x1, waiting for transfers between devices, local(): result = lax.psum_scatter(row_share, 'grp', scatter_dimension=1, tiled=True)  21 us
    dot_general x1, matrix products, local(): jnp.dot(arrived.reshape(-1, pair_cols), blocked, preferred_element_type=j...  17.7 us
  transfers between devices with their start and end apart: 2, of which 2 were waited for; matrix products, arithmetic and copies ran while one was open for 0% of the time, Pallas kernels for 0%

commit v1 on v0

--- a/solution.py
+++ b/solution.py
@@ -11,7 +11,10 @@
     allowed = irrep_ef[:, None] == irrep_ab[None, :]
     blocked = jnp.where(allowed, integrals, jnp.zeros_like(integrals))
     shaped = amplitudes.reshape(own_rows, member_count, pair_cols)
-    arrived = lax.all_to_all(shaped, "mem", split_axis=1, concat_axis=0, tiled=True)
+    n_dev = lax.axis_size("mem")
+    shards = jnp.stack(jnp.split(shaped, n_dev, axis=1), axis=0)
+    shards = lax.all_to_all(shards, "mem", split_axis=0, concat_axis=0)
+    arrived = jnp.concatenate(shards, axis=0)
     partial_value = jnp.dot(
         arrived.reshape(-1, pair_cols), blocked, preferred_element_type=jnp.float32
     )

time: 271 us -> 281 us (1.037)
  local copies, waits for them, and re-layouts: 8.38 us -> 27.7 us
  matrix products: 17.7 us -> 8.16 us
    unnamed x3 -> x2, waiting for transfers between devices: 65.1 us -> 0.03 us
    reduce_scatter x0 -> x1, waiting for transfers between devices: none -> 64.6 us  [local(): lax.psum_scatter(partial_value, 'mem', scatter_dimension=0, tiled=True)]
    split x0 -> x1, local copies, waits for them, and re-layouts: none -> 14.5 us  [local(): shards = jnp.stack(jnp.split(shaped, n_dev, axis=1), axis=0)]
    dot_general x1, matrix products: 17.7 us -> 8.16 us  [local(): jnp.dot(arrived.reshape(-1, pair_cols), blocked, preferred_element_type=j...]
    unnamed x6 -> x20, local copies, waits for them, and re-layouts: 3.58 us -> 12.3 us
    reshape x1 -> x0, local copies, waits for them, and re-layouts: 3.19 us -> none  [local(): shaped = amplitudes.reshape(own_rows, member_count, pair_cols)]
where the time goes in v1:
time: 281 us
  blocking collectives  145 us (52%)
  waiting for transfers between devices  85.7 us (30%)
  local copies, waits for them, and re-layouts  27.7 us (10%)
  between operations  13.6 us (5%)
  matrix products  8.16 us (3%)
    all_to_all x1, blocking collectives, local(): shards = lax.all_to_all(shards, 'mem', split_axis=0, concat_axis=0)  145 us
    reduce_scatter x1, waiting for transfers between devices, local(): lax.psum_scatter(partial_value, 'mem', scatter_dimension=0, tiled=True)  64.6 us
    reduce_scatter x1, waiting for transfers between devices, local(): result = lax.psum_scatter(row_share, 'grp', scatter_dimension=1, tiled=True)  21 us
    split x1, local copies, waits for them, and re-layouts, local(): shards = jnp.stack(jnp.split(shaped, n_dev, axis=1), axis=0)  14.5 us
    unnamed x20, local copies, waits for them, and re-layouts  12.3 us
    dot_general x1, matrix products, local(): jnp.dot(arrived.reshape(-1, pair_cols), blocked, preferred_element_type=j...  8.16 us
  transfers between devices with their start and end apart: 2, of which 2 were waited for; matrix products, arithmetic and copies ran while one was open for 0% of the time, Pallas kernels for 0%

profile of v1, /device:TPU:0, one launch (start us, length us, event | category | flops | bytes accessed | tf_op | source)
XLA Modules:
  0.0 280.6 jit_solution(3707344732023109267)
XLA Ops:
  6.5 6.2 %copy.41 = bf16[6,8,8,8192]{3,2,1,0:T(8,128)(2,1)S(1)} copy(bf16[6,8,8,8192]{3,1,2,0:T(8,128)(2,1)} %bitcast.21) | data formatting | bytes 12582912
  12.8 14.5 %fusion.5 = (bf16[48,1,8192]{2,1,0:T(2,128)(2,1)S(1)}, bf16[48,1,8192]{2,1,0:T(2,128)(2,1)S(1)}, bf16[48,1,8192]{2,1,0:T(2,128)(2,1)S(1)}, bf16[48,1,8192]{2,1,0...) fusion(bf16[48,8,8192]{2,1,0:T(8,128)(2,1)S(1)} %bitcast.20), kind=kLoop, calls=%fused_computation.14 | loop fusion | bytes 12582912 | tf_op jit(solution)/shard_map/split | solution.py:15
  27.3 0.0 slice-start
  27.3 0.9 bitcast_dynamic-update-slice_fusion.7
  28.2 0.9 bitcast_dynamic-update-slice_fusion.6
  29.0 0.9 bitcast_dynamic-update-slice_fusion.5
  29.9 0.0 slice-start.1
  29.9 0.9 bitcast_dynamic-update-slice_fusion.4
  30.8 0.9 bitcast_dynamic-update-slice_fusion.3
  31.7 0.9 bitcast_dynamic-update-slice_fusion.2
  32.5 0.0 slice-start.2
  32.5 0.9 bitcast_dynamic-update-slice_fusion.1
  33.4 0.9 bitcast_dynamic-update-slice_fusion
  34.3 0.0 slice-start.3
  34.3 0.0 copy-start
  34.3 0.0 copy-start.1
  34.3 145.5 %all_to_all.5 = bf16[8,48,1,8192]{3,1,2,0:T(8,128)(2,1)S(1)} all-to-all(bf16[8,48,1,8192]{3,1,2,0:T(8,128)(2,1)S(1)} %bitcast_dynamic-update-slice_fusion), channel_id=1, replica_groups=mesh['grp'=4,'mem'=8] {'mem'}, dimensions={0} | all-to-all | bytes 12582912 | tf_op jit(solution)/shard_map/all_to_all | solution.py:16
  179.8 0.0 slice-done
  179.8 8.2 %fusion = f32[384,1024]{1,0:T(8,128)} fusion(bf16[384,8192]{1,0:T(8,128)(2,1)S(1)} %bitcast.22, bf16[8192,1024]{1,0:T(8,128)(2,1)S(1)} %bitcast.24, s32[1024]{0:T(1024)S(1)} %copy-done.1, s32[8192]{0:T(1024)S(1)} %copy-done), kind=kOutput, calls=%fused_computation.1 | convolution fusion | flops 6459228160 | bytes 24678400 | tf_op jit(solution)/shard_map/dot_general | solution.py:18
  188.0 0.0 reduce-scatter.3.cloned.1.call-update
  188.0 0.0 reduce-scatter.5.cloned.1.call-start
  188.1 64.6 %reduce-scatter.3.cloned.1.call-done = f32[48,1024]{1,0:T(8,128)} async-done(((f32[384,1024]{1,0:T(8,128)}), f32[48,1024]{1,0:T(8,128)}) %reduce-scatter.3.cloned.1.call-update) | async-done | bytes 196624 | tf_op jit(solution)/shard_map/reduce_scatter | solution.py:21
  252.7 0.0 reduce-scatter.5.cloned.1.call-update
  252.7 21.0 %reduce-scatter.5.cloned.1.call-done = f32[48,256]{1,0:T(8,128)} async-done(((f32[48,1024]{1,0:T(8,128)}), f32[48,256]{1,0:T(8,128)}) %reduce-scatter.5.cloned.1.call-update) | async-done | bytes 49168 | tf_op jit(solution)/shard_map/reduce_scatter | solution.py:22
  (7 shorter events, 0.0 us)
Async XLA Ops:
  6.5 246.2 %reduce-scatter.3.cloned.1.call-start = ((), (), s32[]{:S(2)}) async-start(), calls=%async_computation.3 | async-start | bytes 1769472 | tf_op jit(solution)/shard_map/reduce_scatter | solution.py:21
  27.3 152.5 %slice-start = ((s8[16777216]{0:T(1024)(128)(4,1)}), s8[4194304]{0:T(1024)(128)(4,1)S(1)}, s32[]{:S(2)}) async-start(s8[16777216]{0:T(1024)(128)(4,1)} %bitcast.23), calls=%async_computation.5 | async-start | bytes 8388608
  29.9 149.9 %slice-start.1 = ((s8[16777216]{0:T(1024)(128)(4,1)}), s8[4194304]{0:T(1024)(128)(4,1)S(1)}, s32[]{:S(2)}) async-start(s8[16777216]{0:T(1024)(128)(4,1)} %bitcast.23), calls=%async_computation.6 | async-start | bytes 8388608
  32.5 147.3 %slice-start.2 = ((s8[16777216]{0:T(1024)(128)(4,1)}), s8[4194304]{0:T(1024)(128)(4,1)S(1)}, s32[]{:S(2)}) async-start(s8[16777216]{0:T(1024)(128)(4,1)} %bitcast.23), calls=%async_computation.7 | async-start | bytes 8388608
  34.3 145.5 %slice-start.3 = ((s8[16777216]{0:T(1024)(128)(4,1)}), s8[4194304]{0:T(1024)(128)(4,1)S(1)}, s32[]{:S(2)}) async-start(s8[16777216]{0:T(1024)(128)(4,1)} %bitcast.23), calls=%async_computation.8 | async-start | bytes 8388608
  34.3 145.5 %copy-start = (s32[8192]{0:T(1024)S(1)}, s32[8192]{0:T(1024)}, u32[]{:S(2)}) copy-start(s32[8192]{0:T(1024)} %param.6) | copy-start | bytes 98308
  34.3 145.5 %copy-start.1 = (s32[1024]{0:T(1024)S(1)}, s32[1024]{0:T(1024)}, u32[]{:S(2)}) copy-start(s32[1024]{0:T(1024)} %param.7) | copy-start | bytes 12292
  188.0 85.7 %reduce-scatter.5.cloned.1.call-start = ((), (), s32[]{:S(2)}) async-start(), calls=%async_computation.4 | async-start | bytes 245760 | tf_op jit(solution)/shard_map/reduce_scatter | solution.py:22
Sparse Core Ops, SparseCore 0:
  188.2 64.5 reduce-scatter.2
  255.2 18.5 reduce-scatter.4
